TPU v7x, 256 devices: a whole 4x4x8 slice. The times are simulated.
256 devices in a mesh: gx: 8 (over y, core), gy: 4 (over x), gz: 8 (over z).
Axes of the slice: x: 4, y: 4, z: 8, core: 2. Of those that a mesh axis runs over, the one named last changes fastest.
Arguments:
- old_fields: float32 [16384, 4, 512], P(('gx', 'gy', 'gz')), may hold values from 0.5 to 2.5
- new_owner: int32 [16384], P(('gx', 'gy', 'gz')), may hold values from 0 to 63, as said below
- old_owner: int32 [16384], P(('gx', 'gy', 'gz')), may hold values from 0 to 63, as said below
Outputs:
- flame_fields: float32 [4, 128, 64, 1024], P(None, 'gx', 'gy', 'gz')
Inputs may be any that keep to these rules, and one draw needn't show every extreme that they name: A box keeps its gy index; new_owner is the group index of the device of its gx+gz group that holds it after the move. A device sends at most 2 boxes to one device of its group, reaches that number for some device, and every device receives exactly 64 boxes. `old_owner`: agrees with new_owner: the positions of a device naming s are exactly as many as the boxes that device s of the same group and gy sends to it.
All inputs are finite; a program needn't handle non-finite values.
Results may differ from a plain program's by a relative error of at most 0.00002.
Values sent between devices are 32-bit elements; how exact they have to be, the bound alone decides.
A program may use at most 64 MiB of HBM per device.

v0:
```python
import jax
import jax.numpy as jnp
from jax import lax
from jax.sharding import PartitionSpec as P

EDGE = 8
FIELDS = 4
BRICK_X = 2
BRICK_Y = 2
BRICK_Z = 16


DIFFUSION = (1.0, 3.3, 0.9, 1.2)
TIME_STEP = 0.012


def padded(cells, sides, width):
    for axis, dim in sides:
        count = lax.axis_size(axis)
        head = lax.slice_in_dim(cells, 0, width, axis=dim)
        tail = lax.slice_in_dim(cells, cells.shape[dim] - width, cells.shape[dim], axis=dim)
        cells = jnp.concatenate(
            [
                lax.ppermute(tail, axis, [(i, (i + 1) % count) for i in range(count)]),
                cells,
                lax.ppermute(head, axis, [((i + 1) % count, i) for i in range(count)]),
            ],
            axis=dim,
        )
    return cells


def window(array, direction, offset):
    pieces = [slice(None), slice(1, -1), slice(1, -1), slice(1, -1)]
    length = array.shape[direction]
    pieces[direction] = slice(1 + offset, length - 1 + offset)
    return array[tuple(pieces)]


def rates_inside(bordered_fields):
    thermal_field = bordered_fields[0]
    stepping_factors = jnp.array(DIFFUSION, jnp.float32)
    diffusion_coefficient = (
        stepping_factors[:, None, None, None] * (thermal_field * jnp.sqrt(thermal_field))[None]
    )
    centre = bordered_fields[:, 1:-1, 1:-1, 1:-1]
    centre_diffusivity = diffusion_coefficient[:, 1:-1, 1:-1, 1:-1]
    summed = jnp.zeros_like(centre)
    for direction in (1, 2, 3):
        for offset in (1, -1):
            beside = window(bordered_fields, direction, offset)
            beside_diffusivity = window(diffusion_coefficient, direction, offset)
            summed = summed + 0.5 * (centre_diffusivity + beside_diffusivity) * (beside - centre)
    return summed


def with_faces(present_state):
    return padded(present_state, (("gx", 1), ("gy", 2), ("gz", 3)), 1)


def body(old_fields, new_owner, old_owner):
    group_size = lax.axis_size("gx") * lax.axis_size("gz")
    box_count = new_owner.shape[0]
    capacity = 2 * (box_count // group_size)
    positions = jnp.arange(box_count, dtype=jnp.int32)
    earlier = positions[None, :] < positions[:, None]
    sent_rank = jnp.sum(
        ((new_owner[None, :] == new_owner[:, None]) & earlier).astype(jnp.int32), axis=1
    )
    slot_index = new_owner * capacity + sent_rank
    filler = jnp.zeros((group_size * capacity,), jnp.int32).at[slot_index].set(positions)
    departing_boxes = jnp.take(old_fields, filler, axis=0)
    arrived = lax.all_to_all(departing_boxes, ("gx", "gz"), split_axis=0, concat_axis=0, tiled=True)
    holder_position = jnp.sum(
        ((old_owner[None, :] == old_owner[:, None]) & earlier).astype(jnp.int32), axis=1
    )
    box_rows = jnp.take(arrived, old_owner * capacity + holder_position, axis=0)
    present_state = box_rows.reshape(BRICK_X, BRICK_Y, BRICK_Z, FIELDS, EDGE, EDGE, EDGE)
    present_state = present_state.transpose(3, 0, 4, 1, 5, 2, 6).reshape(
        FIELDS, BRICK_X * EDGE, BRICK_Y * EDGE, BRICK_Z * EDGE
    )
    first_section = present_state + TIME_STEP * rates_inside(with_faces(present_state))
    result_fields = 0.5 * present_state + 0.5 * (
        first_section + TIME_STEP * rates_inside(with_faces(first_section))
    )
    return result_fields


def solution(mesh):
    return jax.shard_map(
        body,
        mesh=mesh,
        in_specs=(P(("gx", "gy", "gz"), None, None), P(("gx", "gy", "gz")), P(("gx", "gy", "gz"))),
        out_specs=P(None, "gx", "gy", "gz"),
        check_vma=False,
    )
```

profile of v0, /device:TPU:6, one launch (start us, length us, event | category | flops | bytes accessed | tf_op | source)
XLA Modules:
  0.0 119.7 jit_solution(6868844623129937662)
XLA Ops:
  3.6 1.3 %broadcast_select_fusion = f32[128,4,512]{2,1,0:T(4,128)} fusion(f32[128,4,512]{2,1,0:T(4,128)S(1)} %gather_fusion, pred[128]{0:T(512)(128)(4,1)S(1)} %compare_and_fusion), kind=kLoop, calls=%fused_computation.102 | loop fusion | flops 262144 | bytes 2097280 | tf_op jit(solution)/shard_map/jit(_take)/select_n | solution.py:72
  4.9 12.1 %all-to-all-start = ((f32[128,4,512]{2,1,0:T(4,128)}), f32[128,4,512]{2,1,0:T(4,128)S(1)}, u32[]{:S(2)}, u32[]{:S(2)}) async-start(f32[128,4,512]{2,1,0:T(4,128)} %broadcast_select_fusion), calls=%async_computation | async-start | bytes 2097152 | tf_op jit(solution)/shard_map/all_to_all | solution.py:73
  17.3 28.2 %all-to-all-done = f32[128,4,512]{2,1,0:T(4,128)S(1)} async-done(((f32[128,4,512]{2,1,0:T(4,128)}), f32[128,4,512]{2,1,0:T(4,128)S(1)}, u32[]{:S(2)}, u32[]{:S(2)}) %all-to-all-start) | async-done | bytes 1048608 | tf_op jit(solution)/shard_map/all_to_all | solution.py:73
  46.8 4.7 %gather.12 = f32[2,2,16,4,8,8,8]{2,1,0,6,5,4,3:T(2,128)} reshape(f32[64,4,512]{0,2,1:T(8,128)S(1)} %copy.23) | data formatting | bytes 1048576 | tf_op jit(solution)/shard_map/jit(_take)/gather | solution.py:77
  51.4 7.6 %select_bitcast_fusion = f32[4,2,8,2,8,16,8]{5,3,1,6,4,2,0:T(2,128)} fusion(f32[2,2,16,4,8,8,8]{2,1,0,6,5,4,3:T(2,128)} %gather.12, pred[2,2,16]{2,1,0:T(4,128)(4,1)S(1)} %broadcast_in_dim.42), kind=kLoop, calls=%fused_computation.3 | loop fusion | flops 131072 | bytes 1048640 | tf_op jit(solution)/shard_map/transpose | solution.py:79
  59.0 8.5 %copy.24 = f32[4,2,8,2,8,16,8]{6,5,4,3,2,1,0:T(8,128)} copy(f32[4,2,8,2,8,16,8]{5,3,1,6,4,2,0:T(2,128)} %select_bitcast_fusion) | data formatting | bytes 1048576 | tf_op jit(solution)/shard_map/transpose | solution.py:79
  67.6 6.4 %reshape.23 = f32[4,16,16,128]{3,2,1,0:T(8,128)S(1)} reshape(f32[4,2,8,2,8,16,8]{6,5,4,3,2,1,0:T(8,128)} %copy.24) | data formatting | bytes 1048576 | tf_op jit(solution)/shard_map/reshape | solution.py:79
  74.0 2.9 %collective-permute-start.1 = (f32[4,1,16,128]{3,2,1,0:T(8,128)S(1)}, f32[4,1,16,128]{3,2,1,0:T(8,128)S(1)}, u32[]{:S(2)}, u32[]{:S(2)}) collective-permute-start(f32[4,1,16,128]{3,2,1,0:T(8,128)S(1)} %get-tuple-element.17), channel_id=1, source_target_pairs={{32,0},{64,32},{96,64},{128,96},{160,128},{192,160},{224,192},{0,2... | collective-permute-start | bytes 98312 | tf_op jit(solution)/shard_map/ppermute | solution.py:26
  76.9 1.6 %collective-permute-done = f32[4,1,16,128]{3,2,1,0:T(8,128)S(1)} collective-permute-done((f32[4,1,16,128]{3,2,1,0:T(8,128)S(1)}, f32[4,1,16,128]{3,2,1,0:T(8,128)S(1)}, u32[]{:S(2)}, u32[]{:S(2)}) %collective-permute-start) | collective-permute-done | bytes 32800 | tf_op jit(solution)/shard_map/ppermute | solution.py:24
  79.2 1.5 %collective-permute-start.3 = (f32[4,18,1,128]{3,2,1,0:T(1,128)S(1)}, f32[4,18,1,128]{3,2,1,0:T(1,128)S(1)}, u32[]{:S(2)}, u32[]{:S(2)}) collective-permute-start(f32[4,18,1,128]{3,2,1,0:T(1,128)S(1)} %get-tuple-element.14), channel_id=1, source_target_pairs={{8,0},{16,8},{24,16},{0,24},{9,1},{17,9},{25,17},{1,25},{10,2},{18... | collective-permute-start | bytes 110600 | tf_op jit(solution)/shard_map/ppermute | solution.py:26
  80.8 1.9 %collective-permute-done.2 = f32[4,18,1,128]{3,2,1,0:T(1,128)S(1)} collective-permute-done((f32[4,18,1,128]{3,2,1,0:T(1,128)S(1)}, f32[4,18,1,128]{3,2,1,0:T(1,128)S(1)}, u32[]{:S(2)}, u32[]{:S(2)}) %collective-permute-start.2) | collective-permute-done | bytes 36896 | tf_op jit(solution)/shard_map/ppermute | solution.py:24
  82.7 1.7 %collective-permute-done.3 = f32[4,18,1,128]{3,2,1,0:T(1,128)S(1)} collective-permute-done((f32[4,18,1,128]{3,2,1,0:T(1,128)S(1)}, f32[4,18,1,128]{3,2,1,0:T(1,128)S(1)}, u32[]{:S(2)}, u32[]{:S(2)}) %collective-permute-start.3) | collective-permute-done | bytes 36896 | tf_op jit(solution)/shard_map/ppermute | solution.py:26
  85.4 3.0 %collective-permute-start.5 = (f32[4,18,18,1]{2,0,3,1:T(4,128)S(1)}, f32[4,18,18,1]{2,0,3,1:T(4,128)S(1)}, u32[]{:S(2)}, u32[]{:S(2)}) collective-permute-start(f32[4,18,18,1]{2,0,3,1:T(4,128)S(1)} %copy.26), channel_id=1, source_target_pairs={{1,0},{2,1},{3,2},{4,3},{5,4},{6,5},{7,6},{0,7},{9,8},{10,9},{11,1... | collective-permute-start | bytes 15560 | tf_op jit(solution)/shard_map/ppermute | solution.py:26
  90.6 3.7 %collective-permute-done.4 = f32[4,18,18,1]{2,0,3,1:T(4,128)S(1)} collective-permute-done((f32[4,18,18,1]{2,0,3,1:T(4,128)S(1)}, f32[4,18,18,1]{2,0,3,1:T(4,128)S(1)}, u32[]{:S(2)}, u32[]{:S(2)}) %collective-permute-start.4) | collective-permute-done | bytes 5216 | tf_op jit(solution)/shard_map/ppermute | solution.py:24
  94.9 1.2 %fusion.52 = f32[18,18,130]{2,1,0:T(8,128)S(1)} fusion(f32[4,18,18,1]{3,2,1,0:T(8,128)S(1)} %copy.28, f32[4,18,18,1]{3,2,1,0:T(8,128)S(1)} %copy.27, f32[4,18,1,128]{3,2,1,0:T(1,128)S(1)} %collective-permute-done.3, f32[4,18,16,128]{3,2,1,0:T(8,128)} %copy-done.1, f32[4,18,1,128]{3,2,1,0:T(1,128)S(1)} %collective-permute-done.2), kind=kLoop, calls=%fused_computation.103 | loop fusion | flops 210600 | bytes 842400 | tf_op jit(solution)/shard_map/mul | solution.py:44
  97.2 1.7 %fusion.31 = f32[4,16,16,128]{3,2,1,0:T(8,128)S(1)} fusion(f32[4,16,16,128]{3,2,1,0:T(8,128)S(1)} %reshape.23, f32[4,18,18,1]{3,2,1,0:T(8,128)S(1)} %copy.27, f32[4,18,1,128]{3,2,1,0:T(1,128)S(1)} %collective-permute-done.3, f32[4,18,16,128]{3,2,1,0:T(8,128)S(1)} %copy-done.2, f32[4,18,1,128]{3,2,1,0:T(1,128)S(1)} %collective-permute-done.2, ...), kind=kLoop, calls=%fused_computation.66 | loop fusion | flops 5373952 | bytes 5458048 | tf_op jit(solution)/shard_map/add | solution.py:82
  99.0 2.9 %collective-permute-start.7 = (f32[4,1,16,128]{3,2,1,0:T(8,128)S(1)}, f32[4,1,16,128]{3,2,1,0:T(8,128)S(1)}, u32[]{:S(2)}, u32[]{:S(2)}) collective-permute-start(f32[4,1,16,128]{3,2,1,0:T(8,128)S(1)} %get-tuple-element.16), channel_id=1, source_target_pairs={{32,0},{64,32},{96,64},{128,96},{160,128},{192,160},{224,192},{0,2... | collective-permute-start | bytes 98312 | tf_op jit(solution)/shard_map/ppermute | solution.py:26
  101.9 1.6 %collective-permute-done.6 = f32[4,1,16,128]{3,2,1,0:T(8,128)S(1)} collective-permute-done((f32[4,1,16,128]{3,2,1,0:T(8,128)S(1)}, f32[4,1,16,128]{3,2,1,0:T(8,128)S(1)}, u32[]{:S(2)}, u32[]{:S(2)}) %collective-permute-start.6) | collective-permute-done | bytes 32800 | tf_op jit(solution)/shard_map/ppermute | solution.py:24
  104.0 1.7 %collective-permute-start.9 = (f32[4,18,1,128]{3,2,1,0:T(1,128)S(1)}, f32[4,18,1,128]{3,2,1,0:T(1,128)S(1)}, u32[]{:S(2)}, u32[]{:S(2)}) collective-permute-start(f32[4,18,1,128]{3,2,1,0:T(1,128)S(1)} %get-tuple-element.12), channel_id=1, source_target_pairs={{8,0},{16,8},{24,16},{0,24},{9,1},{17,9},{25,17},{1,25},{10,2},{18... | collective-permute-start | bytes 110600 | tf_op jit(solution)/shard_map/ppermute | solution.py:26
  105.7 1.9 %collective-permute-done.8 = f32[4,18,1,128]{3,2,1,0:T(1,128)S(1)} collective-permute-done((f32[4,18,1,128]{3,2,1,0:T(1,128)S(1)}, f32[4,18,1,128]{3,2,1,0:T(1,128)S(1)}, u32[]{:S(2)}, u32[]{:S(2)}) %collective-permute-start.8) | collective-permute-done | bytes 36896 | tf_op jit(solution)/shard_map/ppermute | solution.py:24
  107.6 1.5 %collective-permute-done.9 = f32[4,18,1,128]{3,2,1,0:T(1,128)S(1)} collective-permute-done((f32[4,18,1,128]{3,2,1,0:T(1,128)S(1)}, f32[4,18,1,128]{3,2,1,0:T(1,128)S(1)}, u32[]{:S(2)}, u32[]{:S(2)}) %collective-permute-start.9) | collective-permute-done | bytes 36896 | tf_op jit(solution)/shard_map/ppermute | solution.py:26
  110.7 2.1 %collective-permute-start.10 = (f32[4,18,18,1]{2,0,3,1:T(4,128)S(1)}, f32[4,18,18,1]{2,0,3,1:T(4,128)S(1)}, u32[]{:S(2)}, u32[]{:S(2)}) collective-permute-start(f32[4,18,18,1]{2,0,3,1:T(4,128)S(1)} %copy.31), channel_id=1, source_target_pairs={{0,1},{1,2},{2,3},{3,4},{4,5},{5,6},{6,7},{7,0},{8,9},{9,10},{10,1... | collective-permute-start | bytes 15560 | tf_op jit(solution)/shard_map/ppermute | solution.py:24
  112.8 1.3 %collective-permute-done.11 = f32[4,18,18,1]{2,0,3,1:T(4,128)S(1)} collective-permute-done((f32[4,18,18,1]{2,0,3,1:T(4,128)S(1)}, f32[4,18,18,1]{2,0,3,1:T(4,128)S(1)}, u32[]{:S(2)}, u32[]{:S(2)}) %collective-permute-start.11) | collective-permute-done | bytes 5216 | tf_op jit(solution)/shard_map/ppermute | solution.py:26
  117.0 2.7 %fusion.6 = f32[4,16,16,128]{3,2,1,0:T(8,128)} fusion(f32[4,16,16,128]{3,2,1,0:T(8,128)S(1)} %reshape.23, f32[4,16,16,128]{3,2,1,0:T(8,128)S(1)} %fusion.31, f32[4,18,18,1]{3,2,1,0:T(8,128)S(1)} %copy.33, f32[4,18,1,128]{3,2,1,0:T(1,128)S(1)} %collective-permute-done.9, f32[4,18,1,128]{3,2,1,0:T(1,128)S(1)} %collective-permute-done.8, ...), kind=kLoop, calls=%fused_computation.17 | loop fusion | flops 6684672 | bytes 5392512 | tf_op jit(solution)/shard_map/add | solution.py:83
  (58 shorter events, 15.4 us)
Async XLA Ops:
  0.0 2.4 %copy-start = (f32[64,4,512]{2,1,0:T(4,128)S(1)}, f32[64,4,512]{2,1,0:T(4,128)}, u32[]{:S(2)}) copy-start(f32[64,4,512]{2,1,0:T(4,128)} %param.5) | copy-start | bytes 1572868
  3.6 13.4 %copy-start.5 = (s32[64]{0:T(128)S(1)}, s32[64]{0:T(128)}, u32[]{:S(2)}) copy-start(s32[64]{0:T(128)} %param.7) | copy-start | bytes 772
  4.9 40.6 %all-to-all-start = ((f32[128,4,512]{2,1,0:T(4,128)}), f32[128,4,512]{2,1,0:T(4,128)S(1)}, u32[]{:S(2)}, u32[]{:S(2)}) async-start(f32[128,4,512]{2,1,0:T(4,128)} %broadcast_select_fusion), calls=%async_computation | async-start | bytes 2097152 | tf_op jit(solution)/shard_map/all_to_all | solution.py:73
  74.0 4.6 %collective-permute-start = (f32[4,1,16,128]{3,2,1,0:T(8,128)S(1)}, f32[4,1,16,128]{3,2,1,0:T(8,128)S(1)}, u32[]{:S(2)}, u32[]{:S(2)}) collective-permute-start(f32[4,1,16,128]{3,2,1,0:T(8,128)S(1)} %get-tuple-element.18), channel_id=1, source_target_pairs={{0,32},{32,64},{64,96},{96,128},{128,160},{160,192},{192,224},{224... | collective-permute-start | bytes 98312 | tf_op jit(solution)/shard_map/ppermute | solution.py:24
  74.0 4.6 %collective-permute-start.1 = (f32[4,1,16,128]{3,2,1,0:T(8,128)S(1)}, f32[4,1,16,128]{3,2,1,0:T(8,128)S(1)}, u32[]{:S(2)}, u32[]{:S(2)}) collective-permute-start(f32[4,1,16,128]{3,2,1,0:T(8,128)S(1)} %get-tuple-element.17), channel_id=1, source_target_pairs={{32,0},{64,32},{96,64},{128,96},{160,128},{192,160},{224,192},{0,2... | collective-permute-start | bytes 98312 | tf_op jit(solution)/shard_map/ppermute | solution.py:26
  78.6 5.8 %copy-start.1 = (f32[4,18,16,128]{3,2,1,0:T(8,128)}, f32[4,18,16,128]{3,2,1,0:T(8,128)S(1)}, u32[]{:S(2)}) copy-start(f32[4,18,16,128]{3,2,1,0:T(8,128)S(1)} %constant_dynamic-update-slice_fusion) | copy-start | bytes 1769476
  78.7 4.1 %collective-permute-start.2 = (f32[4,18,1,128]{3,2,1,0:T(1,128)S(1)}, f32[4,18,1,128]{3,2,1,0:T(1,128)S(1)}, u32[]{:S(2)}, u32[]{:S(2)}) collective-permute-start(f32[4,18,1,128]{3,2,1,0:T(1,128)S(1)} %get-tuple-element.13), channel_id=1, source_target_pairs={{0,8},{8,16},{16,24},{24,0},{1,9},{9,17},{17,25},{25,1},{2,10},{10... | collective-permute-start | bytes 110600 | tf_op jit(solution)/shard_map/ppermute | solution.py:24
  79.2 5.2 %collective-permute-start.3 = (f32[4,18,1,128]{3,2,1,0:T(1,128)S(1)}, f32[4,18,1,128]{3,2,1,0:T(1,128)S(1)}, u32[]{:S(2)}, u32[]{:S(2)}) collective-permute-start(f32[4,18,1,128]{3,2,1,0:T(1,128)S(1)} %get-tuple-element.14), channel_id=1, source_target_pairs={{8,0},{16,8},{24,16},{0,24},{9,1},{17,9},{25,17},{1,25},{10,2},{18... | collective-permute-start | bytes 110600 | tf_op jit(solution)/shard_map/ppermute | solution.py:26
  85.4 4.7 %collective-permute-start.5 = (f32[4,18,18,1]{2,0,3,1:T(4,128)S(1)}, f32[4,18,18,1]{2,0,3,1:T(4,128)S(1)}, u32[]{:S(2)}, u32[]{:S(2)}) collective-permute-start(f32[4,18,18,1]{2,0,3,1:T(4,128)S(1)} %copy.26), channel_id=1, source_target_pairs={{1,0},{2,1},{3,2},{4,3},{5,4},{6,5},{7,6},{0,7},{9,8},{10,9},{11,1... | collective-permute-start | bytes 15560 | tf_op jit(solution)/shard_map/ppermute | solution.py:26
  89.0 5.4 %collective-permute-start.4 = (f32[4,18,18,1]{2,0,3,1:T(4,128)S(1)}, f32[4,18,18,1]{2,0,3,1:T(4,128)S(1)}, u32[]{:S(2)}, u32[]{:S(2)}) collective-permute-start(f32[4,18,18,1]{2,0,3,1:T(4,128)S(1)} %copy.25), channel_id=1, source_target_pairs={{0,1},{1,2},{2,3},{3,4},{4,5},{5,6},{6,7},{7,0},{8,9},{9,10},{10,1... | collective-permute-start | bytes 15560 | tf_op jit(solution)/shard_map/ppermute | solution.py:24
  90.6 5.6 %copy-start.3 = (f32[4]{0:T(128)S(1)}, f32[4]{0:T(128)}, u32[]{:S(2)}) copy-start(f32[4]{0:T(128)} %constant.42.clone) | copy-start | bytes 52
  96.2 1.1 copy-start.2
  99.0 4.6 %collective-permute-start.6 = (f32[4,1,16,128]{3,2,1,0:T(8,128)S(1)}, f32[4,1,16,128]{3,2,1,0:T(8,128)S(1)}, u32[]{:S(2)}, u32[]{:S(2)}) collective-permute-start(f32[4,1,16,128]{3,2,1,0:T(8,128)S(1)} %get-tuple-element.15), channel_id=1, source_target_pairs={{0,32},{32,64},{64,96},{96,128},{128,160},{160,192},{192,224},{224... | collective-permute-start | bytes 98312 | tf_op jit(solution)/shard_map/ppermute | solution.py:24
  99.0 4.5 %collective-permute-start.7 = (f32[4,1,16,128]{3,2,1,0:T(8,128)S(1)}, f32[4,1,16,128]{3,2,1,0:T(8,128)S(1)}, u32[]{:S(2)}, u32[]{:S(2)}) collective-permute-start(f32[4,1,16,128]{3,2,1,0:T(8,128)S(1)} %get-tuple-element.16), channel_id=1, source_target_pairs={{32,0},{64,32},{96,64},{128,96},{160,128},{192,160},{224,192},{0,2... | collective-permute-start | bytes 98312 | tf_op jit(solution)/shard_map/ppermute | solution.py:26
  103.6 4.0 %collective-permute-start.8 = (f32[4,18,1,128]{3,2,1,0:T(1,128)S(1)}, f32[4,18,1,128]{3,2,1,0:T(1,128)S(1)}, u32[]{:S(2)}, u32[]{:S(2)}) collective-permute-start(f32[4,18,1,128]{3,2,1,0:T(1,128)S(1)} %get-tuple-element.11), channel_id=1, source_target_pairs={{0,8},{8,16},{16,24},{24,0},{1,9},{9,17},{17,25},{25,1},{2,10},{10... | collective-permute-start | bytes 110600 | tf_op jit(solution)/shard_map/ppermute | solution.py:24
  104.0 5.2 %collective-permute-start.9 = (f32[4,18,1,128]{3,2,1,0:T(1,128)S(1)}, f32[4,18,1,128]{3,2,1,0:T(1,128)S(1)}, u32[]{:S(2)}, u32[]{:S(2)}) collective-permute-start(f32[4,18,1,128]{3,2,1,0:T(1,128)S(1)} %get-tuple-element.12), channel_id=1, source_target_pairs={{8,0},{16,8},{24,16},{0,24},{9,1},{17,9},{25,17},{1,25},{10,2},{18... | collective-permute-start | bytes 110600 | tf_op jit(solution)/shard_map/ppermute | solution.py:26
  110.1 4.0 %collective-permute-start.11 = (f32[4,18,18,1]{2,0,3,1:T(4,128)S(1)}, f32[4,18,18,1]{2,0,3,1:T(4,128)S(1)}, u32[]{:S(2)}, u32[]{:S(2)}) collective-permute-start(f32[4,18,18,1]{2,0,3,1:T(4,128)S(1)} %copy.32), channel_id=1, source_target_pairs={{1,0},{2,1},{3,2},{4,3},{5,4},{6,5},{7,6},{0,7},{9,8},{10,9},{11,1... | collective-permute-start | bytes 15560 | tf_op jit(solution)/shard_map/ppermute | solution.py:26
  110.7 5.2 %collective-permute-start.10 = (f32[4,18,18,1]{2,0,3,1:T(4,128)S(1)}, f32[4,18,18,1]{2,0,3,1:T(4,128)S(1)}, u32[]{:S(2)}, u32[]{:S(2)}) collective-permute-start(f32[4,18,18,1]{2,0,3,1:T(4,128)S(1)} %copy.31), channel_id=1, source_target_pairs={{0,1},{1,2},{2,3},{3,4},{4,5},{5,6},{6,7},{7,0},{8,9},{9,10},{10,1... | collective-permute-start | bytes 15560 | tf_op jit(solution)/shard_map/ppermute | solution.py:24
  114.7 2.2 %copy-start.4 = (f32[4]{0:T(128)S(1)}, f32[4]{0:T(128)}, u32[]{:S(2)}) copy-start(f32[4]{0:T(128)} %constant.42.clone) | copy-start | bytes 52
where the time goes:
time: 120 us
  waiting for transfers between devices  45.6 us (38%)
  local copies, waits for them, and re-layouts  28.8 us (24%)
  starting transfers between devices  27.7 us (23%)
  other arithmetic  17.4 us (14%)
    all_to_all x1, waiting for transfers between devices, body(): lax.all_to_all(departing_boxes, ('gx', 'gz'), split_axis=0, concat_axis=0...  28.2 us
    ppermute x6, starting transfers between devices, padded(): lax.ppermute(head, axis, [((i + 1) % count, i) for i in range(count)])  12.3 us
    all_to_all x1, starting transfers between devices, body(): lax.all_to_all(departing_boxes, ('gx', 'gz'), split_axis=0, concat_axis=0...  12.1 us
    ppermute x6, waiting for transfers between devices, padded(): lax.ppermute(tail, axis, [(i, (i + 1) % count) for i in range(count)])  12 us
    transpose x1, local copies, waits for them, and re-layouts, body(): present_state.transpose(3, 0, 4, 1, 5, 2, 6)  8.52 us
    transpose x1, other arithmetic, body(): present_state.transpose(3, 0, 4, 1, 5, 2, 6)  7.6 us
    reshape x1, local copies, waits for them, and re-layouts, body(): present_state.transpose(3, 0, 4, 1, 5, 2, 6)  6.37 us
    gather x3, local copies, waits for them, and re-layouts, body(): box_rows = jnp.take(arrived, old_owner * capacity + holder_position, axis=0)  5.88 us
  transfers between devices with their start and end apart: 13, of which 11 were waited for; matrix products, arithmetic and copies ran while one was open for 2% of the time, Pallas kernels for 0%

commit v1 on v0

v1 whole, which is shorter than its diff:
```python
import jax
import jax.numpy as jnp
from jax import lax
from jax.experimental import pallas as pl
from jax.experimental.pallas import tpu as pltpu
from jax.sharding import PartitionSpec as P

DIFFUSION = (1.0, 3.3, 0.9, 1.2)
TIME_STEP = 0.012
MESH = pl.DeviceIdType.MESH
F = 4
PLANE = 16
PAIR = F * 2 * PLANE


def row_of(x, f):
    x = x + 2
    return pl.multiple_of((x // 2) * PAIR + f * 2 * PLANE + (x % 2) * PLANE, PLANE)


def coefficient(t):
    return t * jnp.sqrt(t)


def kernel(
    old_hbm, new_owner, old_owner, out,
    old, send, recv, grid0, grid1, diff, fx, fy, fz, hx, hy, hz, index_v, index_s,
    old_sem, index_sem, send_sem, recv_sem, face_send, face_recv,
):
    gx, gy, gz = lax.axis_index("gx"), lax.axis_index("gy"), lax.axis_index("gz")
    load = pltpu.make_async_copy(old_hbm, old, old_sem)
    load.start()

    barrier = pltpu.get_barrier_semaphore()
    up_y, down_y = (gy + 1) % 4, (gy + 3) % 4
    for y in (up_y, down_y):
        pl.semaphore_signal(barrier, inc=1, device_id={"gy": y}, device_id_type=MESH)

    def peer(r):
        return (gx + r // 8) % 8, (gz + r % 8) % 8

    def greet(r, c):
        px, pz = peer(r)
        pl.semaphore_signal(barrier, inc=1, device_id={"gx": px, "gz": pz}, device_id_type=MESH)
        return c

    lax.fori_loop(1, 64, greet, 0)

    lane = lax.broadcasted_iota(jnp.int32, (8, 128), 1)

    def leaving(i, c):
        first, last = c
        hit = lane == new_owner[i]
        return jnp.where(hit & (first < 0), i, first), jnp.where(hit, i, last)

    none = jnp.full((8, 128), -1, jnp.int32)
    first, last = lax.fori_loop(0, 64, leaving, (none, none))
    index_v[0] = jnp.maximum(first, 0)
    index_v[1] = jnp.maximum(last, 0)
    to_s = pltpu.make_async_copy(index_v.at[pl.ds(0, 2)], index_s.at[pl.ds(0, 2)], index_sem.at[0])
    to_s.start()
    load.wait()
    to_s.wait()

    def pack(r, c):
        px, pz = peer(r)
        owner = px * 8 + pz
        send[2 * r] = old[index_s[0, 0, owner]]
        send[2 * r + 1] = old[index_s[1, 0, owner]]
        return c

    lax.fori_loop(0, 64, pack, 0)
    recv[0] = send[0]
    recv[1] = send[1]
    pl.semaphore_wait(barrier, 65)

    def post(r, c):
        px, pz = peer(r)
        slot = ((8 - r // 8) % 8) * 8 + (8 - r % 8) % 8
        pltpu.make_async_remote_copy(
            src_ref=send.at[pl.ds(2 * r, 2)],
            dst_ref=recv.at[pl.ds(2 * slot, 2)],
            send_sem=send_sem,
            recv_sem=recv_sem,
            device_id={"gx": px, "gz": pz},
            device_id_type=MESH,
        ).start()
        return c

    lax.fori_loop(1, 64, post, 0)

    def owners(i, c):
        return jnp.where(lane == i, old_owner[i], c)

    owner = lax.fori_loop(0, 64, owners, none)

    def ranks(i, c):
        return jnp.where((lane > i) & (owner == old_owner[i]), 1, c)

    rank = lax.fori_loop(0, 64, ranks, jnp.zeros((8, 128), jnp.int32))
    slot = ((owner // 8 - gx + 8) % 8) * 8 + (owner % 8 - gz + 8) % 8
    index_v[2] = slot * 2 + rank
    to_s = pltpu.make_async_copy(index_v.at[pl.ds(2, 1)], index_s.at[pl.ds(2, 1)], index_sem.at[1])
    to_s.start()
    to_s.wait()

    everyone = recv.at[pl.ds(2, 126)]
    pltpu.make_async_copy(everyone, everyone, recv_sem).wait()

    def reorder(s, c):
        bx, by, h = s // 4, (s // 2) % 2, s % 2
        v = [recv[index_s[2, 0, (bx * 2 + by) * 16 + bz], h] for bz in range(16)]
        for step in (1, 2, 4, 8):
            low = ((lane // 8) & step) == 0
            for a in range(16):
                if not a & step:
                    b = a + step
                    v[a], v[b] = (
                        jnp.where(low, v[a], pltpu.roll(v[b], 8 * step, 1)),
                        jnp.where(low, pltpu.roll(v[a], 128 - 8 * step, 1), v[b]),
                    )
        for g in range(16):
            start = (bx * 4 + h * 2 + 1) * PAIR + (g // 8) * PLANE + by * 8 + g % 8
            grid0[pl.ds(start, 8, stride=2 * PLANE), :] = v[g]
        return c

    lax.fori_loop(0, 8, reorder, 0)

    def pack_z(x, f, half, value, ends):
        m = x * 8 + f * 2 + half
        here = lane == m
        return (
            jnp.where(here, pltpu.roll(value, m, 1), ends[0]),
            jnp.where(here, pltpu.roll(value, (m + 1) % 128, 1), ends[1]),
        )

    def exchange(k, grid, ends):
        for side, x in ((0, 0), (1, 15)):
            for f in range(F):
                fx[k, side, pl.ds(f * 16, 16)] = grid[pl.ds(row_of(x, f), 16), :]
        for side, y in ((0, 0), (1, 15)):
            for f in range(F):
                for odd in range(2):
                    fy[k, side, pl.ds((f * 2 + odd) * 8, 8)] = grid[
                        pl.ds(PAIR + (f * 2 + odd) * 16 + y, 8, stride=PAIR), :
                    ]
        for side in range(2):
            fz[k, side] = ends[side]
        copies = []
        for n, (faces, halos, axis, here, size) in enumerate(
            ((fz, hz, "gz", gz, 8), (fy, hy, "gy", gy, 4), (fx, hx, "gx", gx, 8))
        ):
            for side in range(2):
                there = (here + (1 if side else size - 1)) % size
                copy = pltpu.make_async_remote_copy(
                    src_ref=faces.at[k, side],
                    dst_ref=halos.at[k, 1 - side],
                    send_sem=face_send.at[k, n, side],
                    recv_sem=face_recv.at[k, n, 1 - side],
                    device_id={axis: there},
                    device_id_type=MESH,
                )
                copy.start()
                copies.append((copy, n, side))
        for copy, _, _ in copies:
            copy.wait()
        for side, x in ((0, -1), (1, 16)):
            for f in range(F):
                grid[pl.ds(row_of(x, f), 16), :] = hx[k, side, pl.ds(f * 16, 16)]

    sub = lax.broadcasted_iota(jnp.int32, (16, 128), 0)
    wide = lax.broadcasted_iota(jnp.int32, (16, 128), 1)

    def section(k, grid, emit, start):
        def diffusivity(x, c):
            diff[pl.ds(pl.multiple_of(x * 16, 16), 16), :] = coefficient(grid[pl.ds(row_of(x - 1, 0), 16), :])
            return c

        lax.fori_loop(0, 18, diffusivity, 0)
        z_low, z_high = hz[k, 0], hz[k, 1]
        z_low_d, z_high_d = coefficient(z_low), coefficient(z_high)

        def ends_of(low, high, x, f):
            m = x * 8 + f * 2
            return (
                jnp.concatenate([pltpu.roll(low, (128 - m - h) % 128, 1) for h in range(2)], 0),
                jnp.concatenate([pltpu.roll(high, 127 - m - h, 1) for h in range(2)], 0),
            )

        def around(v, low_row, high_row, low_z, high_z):
            return (
                jnp.where(sub == 0, low_row, pltpu.roll(v, 1, 0)),
                jnp.where(sub == 15, high_row, pltpu.roll(v, 15, 0)),
                jnp.where(wide == 0, low_z, pltpu.roll(v, 1, 1)),
                jnp.where(wide == 127, high_z, pltpu.roll(v, 127, 1)),
            )

        def edge_row(side, x, f):
            return hy[k, side, pl.ds((f * 2 + x % 2) * 8 + x // 2, 1), :]

        def plane(x, c):
            d = [diff[pl.ds(pl.multiple_of((x + n) * 16, 16), 16), :] for n in range(3)]
            low_z, high_z = ends_of(z_low_d, z_high_d, x, 0)
            beside = (d[0], d[2]) + around(
                d[1], coefficient(edge_row(0, x, 0)), coefficient(edge_row(1, x, 0)), low_z, high_z
            )
            faces = [(0.5 * TIME_STEP) * (d[1] + n) for n in beside]
            for f in range(F):
                v = grid[pl.ds(row_of(x, f), 16), :]
                low_z, high_z = ends_of(z_low, z_high, x, f)
                near = (
                    grid[pl.ds(row_of(x - 1, f), 16), :],
                    grid[pl.ds(row_of(x + 1, f), 16), :],
                ) + around(v, edge_row(0, x, f), edge_row(1, x, f), low_z, high_z)
                total = faces[0] * (near[0] - v)
                for a, n in zip(faces[1:], near[1:]):
                    total = total + a * (n - v)
                c = emit(x, f, v, DIFFUSION[f] * total, c)
            return c

        return lax.fori_loop(0, 16, plane, start)

    def ends_of_plane(x, f, v, ends):
        for half in range(2):
            ends = pack_z(x, f, half, v[half * 8 : half * 8 + 8], ends)
        return ends

    zero = jnp.zeros((8, 128), jnp.float32)

    def first_ends(x, ends):
        for f in range(F):
            ends = ends_of_plane(x, f, grid0[pl.ds(row_of(x, f), 16), :], ends)
        return ends

    exchange(0, grid0, lax.fori_loop(0, 16, first_ends, (zero, zero)))

    def keep(x, f, v, change, ends):
        w = v + change
        grid1[pl.ds(row_of(x, f), 16), :] = w
        return ends_of_plane(x, f, w, ends)

    exchange(1, grid1, section(0, grid0, keep, (zero, zero)))

    def finish(x, f, w, change, c):
        out[f, x] = 0.5 * grid0[pl.ds(row_of(x, f), 16), :] + 0.5 * (w + change)
        return c

    section(1, grid1, finish, 0)
    sent = send.at[pl.ds(2, 126)]
    pltpu.make_async_copy(sent, sent, send_sem).wait()


def body(old_fields, new_owner, old_owner):
    boxes = old_fields.reshape(64, 4, 4, 128).transpose(0, 2, 1, 3).reshape(64, 2, 8, 128)
    f32 = jnp.float32
    return pl.pallas_call(
        kernel,
        out_shape=jax.ShapeDtypeStruct((F, 16, 16, 128), f32),
        in_specs=[
            pl.BlockSpec(memory_space=pl.ANY),
            pl.BlockSpec(memory_space=pltpu.SMEM),
            pl.BlockSpec(memory_space=pltpu.SMEM),
        ],
        out_specs=pl.BlockSpec(memory_space=pltpu.VMEM),
        scratch_shapes=[
            pltpu.VMEM((64, 2, 8, 128), f32),
            pltpu.VMEM((128, 2, 8, 128), f32),
            pltpu.VMEM((128, 2, 8, 128), f32),
            pltpu.VMEM((10 * PAIR, 128), f32),
            pltpu.VMEM((10 * PAIR, 128), f32),
            pltpu.VMEM((18 * 16, 128), f32),
            pltpu.VMEM((2, 2, 64, 128), f32),
            pltpu.VMEM((2, 2, 64, 128), f32),
            pltpu.VMEM((2, 2, 8, 128), f32),
            pltpu.VMEM((2, 2, 64, 128), f32),
            pltpu.VMEM((2, 2, 64, 128), f32),
            pltpu.VMEM((2, 2, 8, 128), f32),
            pltpu.VMEM((3, 8, 128), jnp.int32),
            pltpu.SMEM((3, 8, 128), jnp.int32),
            pltpu.SemaphoreType.DMA,
            pltpu.SemaphoreType.DMA((2,)),
            pltpu.SemaphoreType.DMA,
            pltpu.SemaphoreType.DMA,
            pltpu.SemaphoreType.DMA((2, 3, 2)),
            pltpu.SemaphoreType.DMA((2, 3, 2)),
        ],
        compiler_params=pltpu.CompilerParams(
            collective_id=0, has_side_effects=True, vmem_limit_bytes=32 * 2**20
        ),
        name="move_and_diffuse",
    )(boxes, new_owner, old_owner)


def solution(mesh):
    return jax.shard_map(
        body,
        mesh=mesh,
        in_specs=(P(("gx", "gy", "gz"), None, None), P(("gx", "gy", "gz")), P(("gx", "gy", "gz"))),
        out_specs=P(None, "gx", "gy", "gz"),
        check_vma=False,
    )
```

time: 120 us -> 57.4 us (0.48)
  the two profiles are of different devices: /device:TPU:6 before, /device:TPU:1 now
where the time goes in v1:
time: 57.4 us; the launch traced here: 57.2 us
  Pallas kernels  54.7 us (95%)
  local copies, waits for them, and re-layouts  2.51 us (4%)
    pallas_call x1, Pallas kernels, body(): pl.pallas_call(kernel, out_shape=jax.ShapeDtypeStruct((F, 16, 16, 128), f...  54.7 us
    unnamed x7, local copies, waits for them, and re-layouts  2.51 us

profile of v1, /device:TPU:1, one launch (start us, length us, event | category | flops | bytes accessed | tf_op | source)
XLA Modules:
  0.0 57.2 jit_solution(2305840616462763268)
XLA Ops:
  0.0 0.0 copy-start.2
  0.0 0.0 copy-start.1
  0.0 0.7 %copy-done.2 = s32[64]{0:T(128)S(1)} copy-done((s32[64]{0:T(128)S(1)}, s32[64]{0:T(128)}, u32[]{:S(2)}) %copy-start.2) | copy-done | bytes 280
  0.7 0.0 copy-done.1
  0.7 0.0 copy-start
  0.7 1.0 %copy-done = f32[64,4,512]{2,1,0:T(4,128)S(1)} copy-done((f32[64,4,512]{2,1,0:T(4,128)S(1)}, f32[64,4,512]{2,1,0:T(4,128)}, u32[]{:S(2)}) %copy-start) | copy-done | bytes 524312
  1.7 54.7 %move_and_diffuse.1 = f32[4,16,16,128]{3,2,1,0:T(8,128)S(1)} custom-call(f32[64,2,8,128]{3,2,1,0:T(8,128)S(1)} %bitcast.5, s32[64]{0:T(128)S(1)} %copy-done.1, s32[64]{0:T(128)S(1)} %copy-done.2), custom_call_target="tpu_custom_call" | custom-call | tf_op jit(solution)/shard_map/move_and_diffuse/pallas_call | solution.py:256
  56.4 0.8 %copy.6 = f32[4,16,16,128]{3,2,1,0:T(8,128)} copy(f32[4,16,16,128]{3,2,1,0:T(8,128)S(1)} %move_and_diffuse.1) | data formatting | bytes 1048576
Async XLA Ops:
  0.0 0.7 %copy-start.2 = (s32[64]{0:T(128)S(1)}, s32[64]{0:T(128)}, u32[]{:S(2)}) copy-start(s32[64]{0:T(128)} %old_owner.1) | copy-start | bytes 772
  0.0 0.7 %copy-start.1 = (s32[64]{0:T(128)S(1)}, s32[64]{0:T(128)}, u32[]{:S(2)}) copy-start(s32[64]{0:T(128)} %new_owner.1) | copy-start | bytes 772
  0.7 1.0 %copy-start = (f32[64,4,512]{2,1,0:T(4,128)S(1)}, f32[64,4,512]{2,1,0:T(4,128)}, u32[]{:S(2)}) copy-start(f32[64,4,512]{2,1,0:T(4,128)} %param.3) | copy-start | bytes 1572868

commit v2 on v0

v2 whole, which is shorter than its diff:
```python
import jax
import jax.numpy as jnp
from jax import lax
from jax.experimental import pallas as pl
from jax.experimental.pallas import tpu as pltpu
from jax.sharding import PartitionSpec as P

DIFFUSION = (1.0, 3.3, 0.9, 1.2)
TIME_STEP = 0.012
MESH = pl.DeviceIdType.MESH
F = 4
CHUNKS = 2
PER = F // CHUNKS
PARTS = (PER + 1) // 2
UNROLL = 2
UNROLL_SETS = 2
SLOT = PER * 8
EDGE = 16
STRIDE = 24
GRID = (EDGE + 2) * STRIDE + 8

OTHERS = sorted(
    [(c, y, z) for c in range(2) for y in range(4) for z in range(8) if c or y or z],
    key=lambda d: -d[0] - min(d[1], 4 - d[1]) - min(d[2], 8 - d[2]),
)


def number(c, y, z):
    return (c * 4 + y % 4) * 8 + z % 8


def coefficient(t):
    return t * jnp.sqrt(t)


def kernel(
    old_hbm, new_hbm, own_hbm, out,
    old, send, recv, grid0, grid1, diff, coef, fy, fz, hy, hz, index_v, index_s, new_owner, old_owner,
    old_sem, owner_sem, index_sem, send_sem, recv_sem, face_send, face_recv,
):
    gx, gy, gz = lax.axis_index("gx"), lax.axis_index("gy"), lax.axis_index("gz")
    core, cy = gx % 2, gx // 2
    grids = (grid0, grid1)

    def peer(c, y, z):
        where = {}
        if c or y:
            where["gx"] = ((cy + y) % 4) * 2 + (core + c) % 2
        if z:
            where["gz"] = (gz + z) % 8
        return where

    barrier = pltpu.get_barrier_semaphore()
    for d in OTHERS:
        pl.semaphore_signal(barrier, inc=1, device_id=peer(*d), device_id_type=MESH)
    for y in (1, 3):
        pl.semaphore_signal(barrier, inc=1, device_id={"gy": (gy + y) % 4}, device_id_type=MESH)
    loads = [
        pltpu.make_async_copy(new_hbm, new_owner, owner_sem.at[0]),
        pltpu.make_async_copy(own_hbm, old_owner, owner_sem.at[1]),
        pltpu.make_async_copy(old_hbm, old.at[pl.ds(16, 1024)], old_sem),
    ]
    for load in loads:
        load.start()
    zeros = jnp.zeros((16, 128), jnp.float32)
    old[pl.ds(0, 16), :] = zeros
    old[pl.ds(1040, 16), :] = zeros
    for k in range(CHUNKS):
        recv[k][pl.ds(0, 8), :] = zeros[:8]
        recv[k][pl.ds(8 + 64 * SLOT, 8), :] = zeros[:8]

    lane = lax.broadcasted_iota(jnp.int32, (8, 128), 1)
    upper = lax.broadcasted_iota(jnp.int32, (8, 128), 0) < 4
    loads[0].wait()

    def leaving(i, c):
        first, last = c
        hit = lane == new_owner[i]
        return jnp.where(hit & (first < 0), i, first), jnp.where(hit, i, last)

    none = jnp.full((8, 128), -1, jnp.int32)
    first, last = lax.fori_loop(0, 64, leaving, (none, none), unroll=8)
    index_v[0] = jnp.maximum(first, 0) * 16
    index_v[1] = jnp.maximum(last, 0) * 16
    to_s = pltpu.make_async_copy(index_v.at[pl.ds(0, 2)], index_s.at[pl.ds(0, 2)], index_sem.at[0])
    to_s.start()
    loads[2].wait()
    to_s.wait()

    def pack(r, c):
        px = ((cy + (r // 8) % 4) % 4) * 2 + (core + r // 32) % 2
        owner = px * 8 + (gz + r) % 8
        a, b = index_s[0, 0, owner], index_s[1, 0, owner]
        for f in range(F):
            va = old[pl.ds(16 + a + f, 8, stride=4), :]
            vb = old[pl.ds(b + f, 8, stride=4), :]
            row = pl.multiple_of(r * SLOT + (f % PER) * 8, 8)
            send[f // PER, pl.ds(row, 8), :] = jnp.where(upper, va, vb)
        return c

    lax.fori_loop(0, 64, pack, 0, unroll=4)
    for k in range(CHUNKS):
        recv[k][pl.ds(8, SLOT), :] = send[k, pl.ds(0, SLOT), :]

    pl.semaphore_wait(barrier, len(OTHERS) + 2)
    for k in range(CHUNKS):
        for c, y, z in OTHERS:
            pltpu.make_async_remote_copy(
                src_ref=send.at[k, pl.ds(number(c, y, z) * SLOT, SLOT)],
                dst_ref=recv[k].at[pl.ds(8 + number(c, -y, -z) * SLOT, SLOT)],
                send_sem=send_sem.at[k],
                recv_sem=recv_sem.at[k],
                device_id=peer(c, y, z),
                device_id_type=MESH,
            ).start()

    loads[1].wait()

    def owners(i, c):
        return jnp.where(lane == i, old_owner[i], c)

    owner = lax.fori_loop(0, 64, owners, none, unroll=8)

    def ranks(i, c):
        return jnp.where((lane > i) & (owner == old_owner[i]), 4, c)

    rank = lax.fori_loop(0, 64, ranks, jnp.zeros((8, 128), jnp.int32), unroll=8)
    ox, oz = owner // 8, owner % 8
    slot = ((ox % 2 - core + 2) % 2 * 4 + (ox // 2 - cy + 4) % 4) * 8 + (oz - gz + 8) % 8
    index_v[2] = slot * SLOT + rank
    to_s = pltpu.make_async_copy(index_v.at[pl.ds(2, 1)], index_s.at[pl.ds(2, 1)], index_sem.at[1])
    to_s.start()
    to_s.wait()

    def arrived(k):
        everyone = recv[k].at[pl.ds(8 + SLOT, 63 * SLOT)]
        pltpu.make_async_copy(everyone, everyone, recv_sem.at[k]).wait()

    bits = [((lane // 8) & step) != 0 for step in (1, 2, 4, 8)]

    def reorder(k):
        def one(s, c):
            f, by = s // 2, s % 2
            v = []
            for bz in range(16):
                a = index_s[2, 0, by * 16 + bz] + f * 8
                b = index_s[2, 0, by * 16 + bz + 32] + f * 8
                box = jnp.where(upper, recv[k][pl.ds(8 + a, 8), :], recv[k][pl.ds(4 + b, 8), :])
                v.append(pltpu.roll(box, 8 * bz, 1) if bz else box)
            for n, bit in enumerate(bits):
                v = [jnp.where(bit, v[(i + (1 << n)) % 16], v[i]) for i in range(16)]
            for g in range(16):
                start = (g // 8 + 1) * STRIDE + 8 + by * 8 + g % 8
                value = pltpu.roll(v[16 - g], 128 - 8 * g, 1) if g else v[0]
                grid0[k * PER + f, pl.ds(start, 8, stride=2 * STRIDE), :] = value
            return c

        lax.fori_loop(0, 2 * PER, one, 0, unroll=UNROLL_SETS)

    def rows(x, y=0):
        if y:
            return pl.ds((x + 1) * STRIDE + 8 + y, EDGE)
        return pl.ds(pl.multiple_of((x + 1) * STRIDE + 8, 8), EDGE)

    def pack_z(x, f, v, ends):
        ends = list(ends)
        for half in range(2):
            twice = (f % 2) * 64 + x * 4 + half * 2
            here = ((lane + 1 - twice) & 127) < 2
            ends[f // 2] = jnp.where(here, pltpu.roll(v[half * 8 : half * 8 + 8], twice, 1), ends[f // 2])
        return tuple(ends)

    def exchange(s, k, ends):
        grid = grids[s]
        fields = pl.ds(k * PER, PER)
        for n, value in enumerate(ends):
            fz[s, k, pl.ds(n * 8, 8)] = value
        copies = []

        def send_face(n, side, axis, here, size, source, target):
            copy = pltpu.make_async_remote_copy(
                src_ref=source,
                dst_ref=target,
                send_sem=face_send.at[s, k, n, side],
                recv_sem=face_recv.at[s, k, n, 1 - side],
                device_id={axis: (here + (1 if side else size - 1)) % size},
                device_id_type=MESH,
            )
            copy.start()
            copies.append(copy)

        for side in range(2):
            send_face(0, side, "gz", gz, 8, fz.at[s, k], hz.at[s, k, 1 - side])
        for side in range(2):
            source = grid.at[fields, pl.ds(STRIDE * (16 if side else 1) + 8, EDGE)]
            target = grid.at[fields, pl.ds(STRIDE * (0 if side else 17) + 8, EDGE)]
            send_face(2, side, "gx", gx, 8, source, target)
        for side in range(2):
            for f in range(PER):
                for part in range(2):
                    fy[s, k, side, pl.ds(f * 16 + part * 8, 8)] = grid[
                        k * PER + f, pl.ds((part * 8 + 1) * STRIDE + 8 + side * 15, 8, stride=STRIDE), :
                    ]
            send_face(1, side, "gy", gy, 4, fy.at[s, k, side], hy.at[s, k, 1 - side])
        everything.extend(copies)
        return copies

    odd = lane % 2 == 1

    def receive(s, k, copies):
        for copy in copies:
            copy.wait_recv()
        for side in range(2):
            for f in range(PER):
                for part in range(2):
                    start = (part * 8 + 1) * STRIDE + (24 if side else 7)
                    grids[s][k * PER + f, pl.ds(start, 8, stride=STRIDE), :] = hy[
                        s, k, side, pl.ds(f * 16 + part * 8, 8)
                    ]
        return [
            jnp.where(odd, hz[s, k, 0, pl.ds(n * 8, 8)], pltpu.roll(hz[s, k, 1, pl.ds(n * 8, 8)], 126, 1))
            for n in range(PARTS)
        ]

    wide = lax.broadcasted_iota(jnp.int32, (16, 128), 1)

    def beside_z(v, edges, x, f):
        twice = (f % 2) * 64 + x * 4
        edge = jnp.concatenate([pltpu.roll(edges[f // 2], (129 - twice - 2 * h) % 128, 1) for h in range(2)], 0)
        return (
            jnp.where(wide == 0, edge, pltpu.roll(v, 1, 1)),
            jnp.where(wide == 127, edge, pltpu.roll(v, 127, 1)),
        )

    def coefficients(s, edges):
        grid = grids[s]

        def diffusivity(x, c):
            part = pl.ds(pl.multiple_of(x * STRIDE, 8), STRIDE)
            diff[part, :] = coefficient(grid[0, part, :])
            return c

        lax.fori_loop(0, 18, diffusivity, 0, unroll=3)
        edges = [coefficient(edge) for edge in edges]

        def plane(x, c):
            d = diff[rows(x), :]
            near = (diff[rows(x - 1), :], diff[rows(x + 1), :], diff[rows(x, -1), :], diff[rows(x, 1), :])
            for n, value in enumerate(near + beside_z(d, edges, x, 0)):
                coef[s, n, pl.ds(pl.multiple_of(x * EDGE, EDGE), EDGE), :] = (0.5 * TIME_STEP) * (d + value)
            return c

        lax.fori_loop(0, 16, plane, 0, unroll=UNROLL)

    def section(s, k, copies, emit, start):
        grid = grids[s]
        edges = receive(s, k, copies)
        if k == 0:
            coefficients(s, edges)

        def plane(x, c):
            faces = [coef[s, n, pl.ds(pl.multiple_of(x * EDGE, EDGE), EDGE), :] for n in range(6)]
            for f in range(PER):
                field = k * PER + f
                v = grid[field, rows(x), :]
                near = (
                    grid[field, rows(x - 1), :],
                    grid[field, rows(x + 1), :],
                    grid[field, rows(x, -1), :],
                    grid[field, rows(x, 1), :],
                ) + beside_z(v, edges, x, f)
                total = faces[0] * (near[0] - v)
                for a, n in zip(faces[1:], near[1:]):
                    total = total + a * (n - v)
                c = emit(x, f, v, DIFFUSION[field] * total, c)
            return c

        return lax.fori_loop(0, 16, plane, start, unroll=UNROLL)

    nothing = (jnp.zeros((8, 128), jnp.float32),) * PARTS
    everything = []

    def to_grid(k):
        arrived(k)
        reorder(k)

        def first_ends(x, ends):
            for f in range(PER):
                ends = pack_z(x, f, grid0[k * PER + f, rows(x), :], ends)
            return ends

        return exchange(0, k, lax.fori_loop(0, 16, first_ends, nothing, unroll=4))

    def first_section(k, copies):
        def keep(x, f, v, change, ends):
            w = v + change
            grid1[k * PER + f, rows(x), :] = w
            return pack_z(x, f, w, ends)

        return exchange(1, k, section(0, k, copies, keep, nothing))

    def second_section(k, copies):
        def finish(x, f, w, change, c):
            out[k * PER + f, x] = 0.5 * grid0[k * PER + f, rows(x), :] + 0.5 * (w + change)
            return c

        section(1, k, copies, finish, 0)

    faces = [to_grid(k) for k in range(CHUNKS)]
    faces = [first_section(k, faces[k]) for k in range(CHUNKS)]
    for k in range(CHUNKS):
        second_section(k, faces[k])
    for copy in everything:
        copy.wait_send()
    for k in range(CHUNKS):
        sent = send.at[k, pl.ds(SLOT, 63 * SLOT)]
        pltpu.make_async_copy(sent, sent, send_sem.at[k]).wait()


def body(old_fields, new_owner, old_owner):
    boxes = old_fields.reshape(64, 4, 4, 128).transpose(0, 2, 1, 3).reshape(1024, 128)
    f32 = jnp.float32
    operands = [pltpu.with_memory_space_constraint(v, pltpu.HBM) for v in (boxes, new_owner, old_owner)]
    return pl.pallas_call(
        kernel,
        out_shape=jax.ShapeDtypeStruct((F, EDGE, EDGE, 128), f32),
        in_specs=[pl.BlockSpec(memory_space=pltpu.HBM)] * 3,
        out_specs=pl.BlockSpec(memory_space=pltpu.VMEM),
        scratch_shapes=[
            pltpu.VMEM((1056, 128), f32),
            pltpu.VMEM((CHUNKS, 64 * SLOT, 128), f32),
            [pltpu.VMEM((64 * SLOT + 16, 128), f32)] * CHUNKS,
            pltpu.VMEM((F, GRID, 128), f32),
            pltpu.VMEM((F, GRID, 128), f32),
            pltpu.VMEM((EDGE * STRIDE + 3 * STRIDE, 128), f32),
            pltpu.VMEM((2, 6, EDGE * EDGE, 128), f32),
            pltpu.VMEM((2, CHUNKS, 2, PER * 16, 128), f32),
            pltpu.VMEM((2, CHUNKS, PARTS * 8, 128), f32),
            pltpu.VMEM((2, CHUNKS, 2, PER * 16, 128), f32),
            pltpu.VMEM((2, CHUNKS, 2, PARTS * 8, 128), f32),
            pltpu.VMEM((3, 8, 128), jnp.int32),
            pltpu.SMEM((3, 8, 128), jnp.int32),
            pltpu.SMEM((64,), jnp.int32),
            pltpu.SMEM((64,), jnp.int32),
            pltpu.SemaphoreType.DMA,
            pltpu.SemaphoreType.DMA((2,)),
            pltpu.SemaphoreType.DMA((2,)),
            pltpu.SemaphoreType.DMA((CHUNKS,)),
            pltpu.SemaphoreType.DMA((CHUNKS,)),
            pltpu.SemaphoreType.DMA((2, CHUNKS, 3, 2)),
            pltpu.SemaphoreType.DMA((2, CHUNKS, 3, 2)),
        ],
        compiler_params=pltpu.CompilerParams(
            collective_id=0, has_side_effects=True, vmem_limit_bytes=32 * 2**20
        ),
        name="move_and_diffuse",
    )(*operands)


def solution(mesh):
    return jax.shard_map(
        body,
        mesh=mesh,
        in_specs=(P(("gx", "gy", "gz"), None, None), P(("gx", "gy", "gz")), P(("gx", "gy", "gz"))),
        out_specs=P(None, "gx", "gy", "gz"),
        check_vma=False,
    )
```

time: 120 us -> 47.6 us (0.40)
  the two profiles are of different devices: /device:TPU:6 before, /device:TPU:1 now
where the time goes in v2:
time: 47.6 us; the launch traced here: 47.5 us
  Pallas kernels  46.7 us (98%)
  local copies, waits for them, and re-layouts  0.8 us (2%)
    pallas_call x1, Pallas kernels, body(): pl.pallas_call(kernel, out_shape=jax.ShapeDtypeStruct((F, EDGE, EDGE, 128...  46.7 us

profile of v2, /device:TPU:1, one launch (start us, length us, event | category | flops | bytes accessed | tf_op | source)
XLA Modules:
  0.0 47.5 jit_solution(16444951422959479370)
XLA Ops:
  0.0 46.7 %move_and_diffuse.1 = f32[4,16,16,128]{3,2,1,0:T(8,128)S(1)} custom-call(f32[1024,128]{1,0:T(8,128)} %bitcast.5, s32[64]{0:T(128)} %new_hbm.1, s32[64]{0:T(128)} %own_hbm.1), custom_call_target="tpu_custom_call" | custom-call | tf_op jit(solution)/shard_map/move_and_diffuse/pallas_call | solution.py:324
  46.7 0.8 %copy.6 = f32[4,16,16,128]{3,2,1,0:T(8,128)} copy(f32[4,16,16,128]{3,2,1,0:T(8,128)S(1)} %move_and_diffuse.1) | data formatting | bytes 1048576

commit v3 on v2

--- a/solution.py
+++ b/solution.py
@@ -9,12 +9,11 @@
 TIME_STEP = 0.012
 MESH = pl.DeviceIdType.MESH
 F = 4
-CHUNKS = 2
-PER = F // CHUNKS
-PARTS = (PER + 1) // 2
-UNROLL = 2
-UNROLL_SETS = 2
-SLOT = PER * 8
+FIELDS = ((0, 1, 2), (3,))
+CHUNKS = len(FIELDS)
+SLOT = [8 * len(fields) for fields in FIELDS]
+PARTS = [(len(fields) + 1) // 2 for fields in FIELDS]
+UNROLL = 8
 EDGE = 16
 STRIDE = 24
 GRID = (EDGE + 2) * STRIDE + 8
@@ -67,7 +66,7 @@
     old[pl.ds(1040, 16), :] = zeros
     for k in range(CHUNKS):
         recv[k][pl.ds(0, 8), :] = zeros[:8]
-        recv[k][pl.ds(8 + 64 * SLOT, 8), :] = zeros[:8]
+        recv[k][pl.ds(8 + 64 * SLOT[k], 8), :] = zeros[:8]
 
     lane = lax.broadcasted_iota(jnp.int32, (8, 128), 1)
     upper = lax.broadcasted_iota(jnp.int32, (8, 128), 0) < 4
@@ -94,20 +93,21 @@
         for f in range(F):
             va = old[pl.ds(16 + a + f, 8, stride=4), :]
             vb = old[pl.ds(b + f, 8, stride=4), :]
-            row = pl.multiple_of(r * SLOT + (f % PER) * 8, 8)
-            send[f // PER, pl.ds(row, 8), :] = jnp.where(upper, va, vb)
+            k = next(k for k in range(CHUNKS) if f in FIELDS[k])
+            row = pl.multiple_of(r * SLOT[k] + FIELDS[k].index(f) * 8, 8)
+            send[k][pl.ds(row, 8), :] = jnp.where(upper, va, vb)
         return c
 
     lax.fori_loop(0, 64, pack, 0, unroll=4)
     for k in range(CHUNKS):
-        recv[k][pl.ds(8, SLOT), :] = send[k, pl.ds(0, SLOT), :]
+        recv[k][pl.ds(8, SLOT[k]), :] = send[k][pl.ds(0, SLOT[k]), :]
 
     pl.semaphore_wait(barrier, len(OTHERS) + 2)
     for k in range(CHUNKS):
         for c, y, z in OTHERS:
             pltpu.make_async_remote_copy(
-                src_ref=send.at[k, pl.ds(number(c, y, z) * SLOT, SLOT)],
-                dst_ref=recv[k].at[pl.ds(8 + number(c, -y, -z) * SLOT, SLOT)],
+                src_ref=send[k].at[pl.ds(number(c, y, z) * SLOT[k], SLOT[k])],
+                dst_ref=recv[k].at[pl.ds(8 + number(c, -y, -z) * SLOT[k], SLOT[k])],
                 send_sem=send_sem.at[k],
                 recv_sem=recv_sem.at[k],
                 device_id=peer(c, y, z),
@@ -127,13 +127,16 @@
     rank = lax.fori_loop(0, 64, ranks, jnp.zeros((8, 128), jnp.int32), unroll=8)
     ox, oz = owner // 8, owner % 8
     slot = ((ox % 2 - core + 2) % 2 * 4 + (ox // 2 - cy + 4) % 4) * 8 + (oz - gz + 8) % 8
-    index_v[2] = slot * SLOT + rank
-    to_s = pltpu.make_async_copy(index_v.at[pl.ds(2, 1)], index_s.at[pl.ds(2, 1)], index_sem.at[1])
+    for k in range(CHUNKS):
+        index_v[2 + k] = slot * SLOT[k] + rank
+    to_s = pltpu.make_async_copy(
+        index_v.at[pl.ds(2, CHUNKS)], index_s.at[pl.ds(2, CHUNKS)], index_sem.at[1]
+    )
     to_s.start()
     to_s.wait()
 
     def arrived(k):
-        everyone = recv[k].at[pl.ds(8 + SLOT, 63 * SLOT)]
+        everyone = recv[k].at[pl.ds(8 + SLOT[k], 63 * SLOT[k])]
         pltpu.make_async_copy(everyone, everyone, recv_sem.at[k]).wait()
 
     bits = [((lane // 8) & step) != 0 for step in (1, 2, 4, 8)]
@@ -143,8 +146,8 @@
             f, by = s // 2, s % 2
             v = []
             for bz in range(16):
-                a = index_s[2, 0, by * 16 + bz] + f * 8
-                b = index_s[2, 0, by * 16 + bz + 32] + f * 8
+                a = index_s[2 + k, 0, by * 16 + bz] + f * 8
+                b = index_s[2 + k, 0, by * 16 + bz + 32] + f * 8
                 box = jnp.where(upper, recv[k][pl.ds(8 + a, 8), :], recv[k][pl.ds(4 + b, 8), :])
                 v.append(pltpu.roll(box, 8 * bz, 1) if bz else box)
             for n, bit in enumerate(bits):
@@ -152,10 +155,10 @@
             for g in range(16):
                 start = (g // 8 + 1) * STRIDE + 8 + by * 8 + g % 8
                 value = pltpu.roll(v[16 - g], 128 - 8 * g, 1) if g else v[0]
-                grid0[k * PER + f, pl.ds(start, 8, stride=2 * STRIDE), :] = value
-            return c
-
-        lax.fori_loop(0, 2 * PER, one, 0, unroll=UNROLL_SETS)
+                grid0[FIELDS[k][0] + f, pl.ds(start, 8, stride=2 * STRIDE), :] = value
+            return c
+
+        lax.fori_loop(0, 2 * len(FIELDS[k]), one, 0, unroll=2)
 
     def rows(x, y=0):
         if y:
@@ -172,9 +175,9 @@
 
     def exchange(s, k, ends):
         grid = grids[s]
-        fields = pl.ds(k * PER, PER)
+        fields = pl.ds(FIELDS[k][0], len(FIELDS[k]))
         for n, value in enumerate(ends):
-            fz[s, k, pl.ds(n * 8, 8)] = value
+            fz[k][s, pl.ds(n * 8, 8)] = value
         copies = []
 
         def send_face(n, side, axis, here, size, source, target):
@@ -190,18 +193,18 @@
             copies.append(copy)
 
         for side in range(2):
-            send_face(0, side, "gz", gz, 8, fz.at[s, k], hz.at[s, k, 1 - side])
+            send_face(0, side, "gz", gz, 8, fz[k].at[s], hz[k].at[s, 1 - side])
         for side in range(2):
             source = grid.at[fields, pl.ds(STRIDE * (16 if side else 1) + 8, EDGE)]
             target = grid.at[fields, pl.ds(STRIDE * (0 if side else 17) + 8, EDGE)]
             send_face(2, side, "gx", gx, 8, source, target)
         for side in range(2):
-            for f in range(PER):
+            for f, field in enumerate(FIELDS[k]):
                 for part in range(2):
-                    fy[s, k, side, pl.ds(f * 16 + part * 8, 8)] = grid[
-                        k * PER + f, pl.ds((part * 8 + 1) * STRIDE + 8 + side * 15, 8, stride=STRIDE), :
+                    fy[k][s, side, pl.ds(f * 16 + part * 8, 8)] = grid[
+                        field, pl.ds((part * 8 + 1) * STRIDE + 8 + side * 15, 8, stride=STRIDE), :
                     ]
-            send_face(1, side, "gy", gy, 4, fy.at[s, k, side], hy.at[s, k, 1 - side])
+            send_face(1, side, "gy", gy, 4, fy[k].at[s, side], hy[k].at[s, 1 - side])
         everything.extend(copies)
         return copies
 
@@ -211,15 +214,15 @@
         for copy in copies:
             copy.wait_recv()
         for side in range(2):
-            for f in range(PER):
+            for f, field in enumerate(FIELDS[k]):
                 for part in range(2):
                     start = (part * 8 + 1) * STRIDE + (24 if side else 7)
-                    grids[s][k * PER + f, pl.ds(start, 8, stride=STRIDE), :] = hy[
-                        s, k, side, pl.ds(f * 16 + part * 8, 8)
+                    grids[s][field, pl.ds(start, 8, stride=STRIDE), :] = hy[k][
+                        s, side, pl.ds(f * 16 + part * 8, 8)
                     ]
         return [
-            jnp.where(odd, hz[s, k, 0, pl.ds(n * 8, 8)], pltpu.roll(hz[s, k, 1, pl.ds(n * 8, 8)], 126, 1))
-            for n in range(PARTS)
+            jnp.where(odd, hz[k][s, 0, pl.ds(n * 8, 8)], pltpu.roll(hz[k][s, 1, pl.ds(n * 8, 8)], 126, 1))
+            for n in range(PARTS[k])
         ]
 
     wide = lax.broadcasted_iota(jnp.int32, (16, 128), 1)
@@ -260,8 +263,7 @@
 
         def plane(x, c):
             faces = [coef[s, n, pl.ds(pl.multiple_of(x * EDGE, EDGE), EDGE), :] for n in range(6)]
-            for f in range(PER):
-                field = k * PER + f
+            for f, field in enumerate(FIELDS[k]):
                 v = grid[field, rows(x), :]
                 near = (
                     grid[field, rows(x - 1), :],
@@ -272,12 +274,12 @@
                 total = faces[0] * (near[0] - v)
                 for a, n in zip(faces[1:], near[1:]):
                     total = total + a * (n - v)
-                c = emit(x, f, v, DIFFUSION[field] * total, c)
+                c = emit(x, f, field, v, DIFFUSION[field] * total, c)
             return c
 
         return lax.fori_loop(0, 16, plane, start, unroll=UNROLL)
 
-    nothing = (jnp.zeros((8, 128), jnp.float32),) * PARTS
+    nothing = [(jnp.zeros((8, 128), jnp.float32),) * PARTS[k] for k in range(CHUNKS)]
     everything = []
 
     def to_grid(k):
@@ -285,23 +287,23 @@
         reorder(k)
 
         def first_ends(x, ends):
-            for f in range(PER):
-                ends = pack_z(x, f, grid0[k * PER + f, rows(x), :], ends)
+            for f, field in enumerate(FIELDS[k]):
+                ends = pack_z(x, f, grid0[field, rows(x), :], ends)
             return ends
 
-        return exchange(0, k, lax.fori_loop(0, 16, first_ends, nothing, unroll=4))
+        return exchange(0, k, lax.fori_loop(0, 16, first_ends, nothing[k], unroll=4))
 
     def first_section(k, copies):
-        def keep(x, f, v, change, ends):
+        def keep(x, f, field, v, change, ends):
             w = v + change
-            grid1[k * PER + f, rows(x), :] = w
+            grid1[field, rows(x), :] = w
             return pack_z(x, f, w, ends)
 
-        return exchange(1, k, section(0, k, copies, keep, nothing))
+        return exchange(1, k, section(0, k, copies, keep, nothing[k]))
 
     def second_section(k, copies):
-        def finish(x, f, w, change, c):
-            out[k * PER + f, x] = 0.5 * grid0[k * PER + f, rows(x), :] + 0.5 * (w + change)
+        def finish(x, f, field, w, change, c):
+            out[field, x] = 0.5 * grid0[field, rows(x), :] + 0.5 * (w + change)
             return c
 
         section(1, k, copies, finish, 0)
@@ -313,7 +315,7 @@
     for copy in everything:
         copy.wait_send()
     for k in range(CHUNKS):
-        sent = send.at[k, pl.ds(SLOT, 63 * SLOT)]
+        sent = send[k].at[pl.ds(SLOT[k], 63 * SLOT[k])]
         pltpu.make_async_copy(sent, sent, send_sem.at[k]).wait()
 
 
@@ -328,18 +330,18 @@
         out_specs=pl.BlockSpec(memory_space=pltpu.VMEM),
         scratch_shapes=[
             pltpu.VMEM((1056, 128), f32),
-            pltpu.VMEM((CHUNKS, 64 * SLOT, 128), f32),
-            [pltpu.VMEM((64 * SLOT + 16, 128), f32)] * CHUNKS,
+            [pltpu.VMEM((64 * rows, 128), f32) for rows in SLOT],
+            [pltpu.VMEM((64 * rows + 16, 128), f32) for rows in SLOT],
             pltpu.VMEM((F, GRID, 128), f32),
             pltpu.VMEM((F, GRID, 128), f32),
             pltpu.VMEM((EDGE * STRIDE + 3 * STRIDE, 128), f32),
             pltpu.VMEM((2, 6, EDGE * EDGE, 128), f32),
-            pltpu.VMEM((2, CHUNKS, 2, PER * 16, 128), f32),
-            pltpu.VMEM((2, CHUNKS, PARTS * 8, 128), f32),
-            pltpu.VMEM((2, CHUNKS, 2, PER * 16, 128), f32),
-            pltpu.VMEM((2, CHUNKS, 2, PARTS * 8, 128), f32),
-            pltpu.VMEM((3, 8, 128), jnp.int32),
-            pltpu.SMEM((3, 8, 128), jnp.int32),
+            [pltpu.VMEM((2, 2, rows * 2, 128), f32) for rows in SLOT],
+            [pltpu.VMEM((2, parts * 8, 128), f32) for parts in PARTS],
+            [pltpu.VMEM((2, 2, rows * 2, 128), f32) for rows in SLOT],
+            [pltpu.VMEM((2, 2, parts * 8, 128), f32) for parts in PARTS],
+            pltpu.VMEM((2 + CHUNKS, 8, 128), jnp.int32),
+            pltpu.SMEM((2 + CHUNKS, 8, 128), jnp.int32),
             pltpu.SMEM((64,), jnp.int32),
             pltpu.SMEM((64,), jnp.int32),
             pltpu.SemaphoreType.DMA,

time: 47.6 us -> 45.4 us (0.954)
  Pallas kernels: 46.7 us -> 44.5 us
    pallas_call x1, Pallas kernels: 46.7 us -> 44.5 us  [body(): pl.pallas_call(kernel, out_shape=jax.ShapeDtypeStruct((F, EDGE, EDGE, 128...]
where the time goes in v3:
time: 45.4 us; the launch traced here: 45.3 us
  Pallas kernels  44.5 us (98%)
  local copies, waits for them, and re-layouts  0.8 us (2%)
    pallas_call x1, Pallas kernels, body(): pl.pallas_call(kernel, out_shape=jax.ShapeDtypeStruct((F, EDGE, EDGE, 128...  44.5 us

profile of v3, /device:TPU:1, one launch (start us, length us, event | category | flops | bytes accessed | tf_op | source)
XLA Modules:
  0.0 45.3 jit_solution(484912484114611144)
XLA Ops:
  0.0 44.5 %move_and_diffuse.1 = f32[4,16,16,128]{3,2,1,0:T(8,128)S(1)} custom-call(f32[1024,128]{1,0:T(8,128)} %bitcast.5, s32[64]{0:T(128)} %new_hbm.1, s32[64]{0:T(128)} %own_hbm.1), custom_call_target="tpu_custom_call" | custom-call | tf_op jit(solution)/shard_map/move_and_diffuse/pallas_call | solution.py:326
  44.5 0.8 %copy.6 = f32[4,16,16,128]{3,2,1,0:T(8,128)} copy(f32[4,16,16,128]{3,2,1,0:T(8,128)S(1)} %move_and_diffuse.1) | data formatting | bytes 1048576

commit v4 on v3

--- a/solution.py
+++ b/solution.py
@@ -24,6 +24,18 @@
 )
 
 
+def hops(c, y, z):
+    return c + min(y, 4 - y) + min(z, 8 - z)
+
+
+def ball(n):
+    return [d for d in OTHERS if hops(*d) <= n]
+
+
+GREET = (2, 2, 3)
+KNOWN = (2, 4, 7)
+
+
 def number(c, y, z):
     return (c * 4 + y % 4) * 8 + z % 8
 
@@ -35,7 +47,7 @@
 def kernel(
     old_hbm, new_hbm, own_hbm, out,
     old, send, recv, grid0, grid1, diff, coef, fy, fz, hy, hz, index_v, index_s, new_owner, old_owner,
-    old_sem, owner_sem, index_sem, send_sem, recv_sem, face_send, face_recv,
+    old_sem, owner_sem, index_sem, ready, send_sem, recv_sem, face_send, face_recv,
 ):
     gx, gy, gz = lax.axis_index("gx"), lax.axis_index("gy"), lax.axis_index("gz")
     core, cy = gx % 2, gx // 2
@@ -50,8 +62,11 @@
         return where
 
     barrier = pltpu.get_barrier_semaphore()
-    for d in OTHERS:
-        pl.semaphore_signal(barrier, inc=1, device_id=peer(*d), device_id_type=MESH)
+    def greet(sem, r):
+        for d in ball(GREET[r]):
+            pl.semaphore_signal(sem, inc=1, device_id=peer(*d), device_id_type=MESH)
+
+    greet(barrier, 0)
     for y in (1, 3):
         pl.semaphore_signal(barrier, inc=1, device_id={"gy": (gy + y) % 4}, device_id_type=MESH)
     loads = [
@@ -102,9 +117,10 @@
     for k in range(CHUNKS):
         recv[k][pl.ds(8, SLOT[k]), :] = send[k][pl.ds(0, SLOT[k]), :]
 
-    pl.semaphore_wait(barrier, len(OTHERS) + 2)
-    for k in range(CHUNKS):
+    def post(k, near, far):
         for c, y, z in OTHERS:
+            if not near < hops(c, y, z) <= far:
+                continue
             pltpu.make_async_remote_copy(
                 src_ref=send[k].at[pl.ds(number(c, y, z) * SLOT[k], SLOT[k])],
                 dst_ref=recv[k].at[pl.ds(8 + number(c, -y, -z) * SLOT[k], SLOT[k])],
@@ -113,6 +129,19 @@
                 device_id=peer(c, y, z),
                 device_id_type=MESH,
             ).start()
+
+    last = len(KNOWN) - 1
+    for r, far in enumerate(KNOWN):
+        if r:
+            pl.semaphore_wait(ready.at[r - 1], len(ball(GREET[r])))
+        else:
+            pl.semaphore_wait(barrier, len(ball(GREET[0])) + 2)
+        if r < last:
+            greet(ready.at[r], r + 1)
+        post(0, KNOWN[r - 1] if r else 0, far)
+        if r == 0:
+            post(1, 0, 2)
+    post(1, 2, 7)
 
     loads[1].wait()
 
@@ -176,8 +205,6 @@
     def exchange(s, k, ends):
         grid = grids[s]
         fields = pl.ds(FIELDS[k][0], len(FIELDS[k]))
-        for n, value in enumerate(ends):
-            fz[k][s, pl.ds(n * 8, 8)] = value
         copies = []
 
         def send_face(n, side, axis, here, size, source, target):
@@ -193,8 +220,6 @@
             copies.append(copy)
 
         for side in range(2):
-            send_face(0, side, "gz", gz, 8, fz[k].at[s], hz[k].at[s, 1 - side])
-        for side in range(2):
             source = grid.at[fields, pl.ds(STRIDE * (16 if side else 1) + 8, EDGE)]
             target = grid.at[fields, pl.ds(STRIDE * (0 if side else 17) + 8, EDGE)]
             send_face(2, side, "gx", gx, 8, source, target)
@@ -205,6 +230,12 @@
                         field, pl.ds((part * 8 + 1) * STRIDE + 8 + side * 15, 8, stride=STRIDE), :
                     ]
             send_face(1, side, "gy", gy, 4, fy[k].at[s, side], hy[k].at[s, 1 - side])
+        if callable(ends):
+            ends = ends()
+        for n, value in enumerate(ends):
+            fz[k][s, pl.ds(n * 8, 8)] = value
+        for side in range(2):
+            send_face(0, side, "gz", gz, 8, fz[k].at[s], hz[k].at[s, 1 - side])
         everything.extend(copies)
         return copies
 
@@ -291,7 +322,7 @@
                 ends = pack_z(x, f, grid0[field, rows(x), :], ends)
             return ends
 
-        return exchange(0, k, lax.fori_loop(0, 16, first_ends, nothing[k], unroll=4))
+        return exchange(0, k, lambda: lax.fori_loop(0, 16, first_ends, nothing[k], unroll=4))
 
     def first_section(k, copies):
         def keep(x, f, field, v, change, ends):
@@ -347,6 +378,7 @@
             pltpu.SemaphoreType.DMA,
             pltpu.SemaphoreType.DMA((2,)),
             pltpu.SemaphoreType.DMA((2,)),
+            pltpu.SemaphoreType.REGULAR((len(KNOWN),)),
             pltpu.SemaphoreType.DMA((CHUNKS,)),
             pltpu.SemaphoreType.DMA((CHUNKS,)),
             pltpu.SemaphoreType.DMA((2, CHUNKS, 3, 2)),

time: 45.4 us -> 44.6 us (0.982)
  Pallas kernels: 44.5 us -> 43.7 us
    pallas_call x1, Pallas kernels: 44.5 us -> 43.7 us  [body(): pl.pallas_call(kernel, out_shape=jax.ShapeDtypeStruct((F, EDGE, EDGE, 128...]
where the time goes in v4:
time: 44.6 us; the launch traced here: 44.5 us
  Pallas kernels  43.7 us (98%)
  local copies, waits for them, and re-layouts  0.8 us (2%)
    pallas_call x1, Pallas kernels, body(): pl.pallas_call(kernel, out_shape=jax.ShapeDtypeStruct((F, EDGE, EDGE, 128...  43.7 us

profile of v4, /device:TPU:1, one launch (start us, length us, event | category | flops | bytes accessed | tf_op | source)
XLA Modules:
  0.0 44.5 jit_solution(5048216039014021087)
XLA Ops:
  0.0 43.7 %move_and_diffuse.1 = f32[4,16,16,128]{3,2,1,0:T(8,128)S(1)} custom-call(f32[1024,128]{1,0:T(8,128)} %bitcast.5, s32[64]{0:T(128)} %new_hbm.1, s32[64]{0:T(128)} %own_hbm.1), custom_call_target="tpu_custom_call" | custom-call | tf_op jit(solution)/shard_map/move_and_diffuse/pallas_call | solution.py:357
  43.7 0.8 %copy.6 = f32[4,16,16,128]{3,2,1,0:T(8,128)} copy(f32[4,16,16,128]{3,2,1,0:T(8,128)S(1)} %move_and_diffuse.1) | data formatting | bytes 1048576

commit v5 on v4

--- a/solution.py
+++ b/solution.py
@@ -308,7 +308,7 @@
                 c = emit(x, f, field, v, DIFFUSION[field] * total, c)
             return c
 
-        return lax.fori_loop(0, 16, plane, start, unroll=UNROLL)
+        return lax.fori_loop(0, 16, plane, start, unroll=16 if k else UNROLL)
 
     nothing = [(jnp.zeros((8, 128), jnp.float32),) * PARTS[k] for k in range(CHUNKS)]
     everything = []
@@ -322,7 +322,7 @@
                 ends = pack_z(x, f, grid0[field, rows(x), :], ends)
             return ends
 
-        return exchange(0, k, lambda: lax.fori_loop(0, 16, first_ends, nothing[k], unroll=4))
+        return exchange(0, k, lambda: lax.fori_loop(0, 16, first_ends, nothing[k], unroll=16 if k else 4))
 
     def first_section(k, copies):
         def keep(x, f, field, v, change, ends):
@@ -339,15 +339,21 @@
 
         section(1, k, copies, finish, 0)
 
+    def settle():
+        for copy in everything[: len(everything) - 6]:
+            copy.wait_send()
+        for k in range(CHUNKS):
+            sent = send[k].at[pl.ds(SLOT[k], 63 * SLOT[k])]
+            pltpu.make_async_copy(sent, sent, send_sem.at[k]).wait()
+
     faces = [to_grid(k) for k in range(CHUNKS)]
     faces = [first_section(k, faces[k]) for k in range(CHUNKS)]
-    for k in range(CHUNKS):
+    for k in range(CHUNKS - 1):
         second_section(k, faces[k])
-    for copy in everything:
+    settle()
+    second_section(CHUNKS - 1, faces[-1])
+    for copy in everything[-6:]:
         copy.wait_send()
-    for k in range(CHUNKS):
-        sent = send[k].at[pl.ds(SLOT[k], 63 * SLOT[k])]
-        pltpu.make_async_copy(sent, sent, send_sem.at[k]).wait()
 
 
 def body(old_fields, new_owner, old_owner):

time: 44.6 us -> 44.1 us (0.989)
  Pallas kernels: 43.7 us -> 43.2 us
    pallas_call x1, Pallas kernels: 43.7 us -> 43.2 us  [body(): pl.pallas_call(kernel, out_shape=jax.ShapeDtypeStruct((F, EDGE, EDGE, 128...]
where the time goes in v5:
time: 44.1 us; the launch traced here: 44 us
  Pallas kernels  43.2 us (98%)
  local copies, waits for them, and re-layouts  0.8 us (2%)
    pallas_call x1, Pallas kernels, body(): pl.pallas_call(kernel, out_shape=jax.ShapeDtypeStruct((F, EDGE, EDGE, 128...  43.2 us

profile of v5, /device:TPU:1, one launch (start us, length us, event | category | flops | bytes accessed | tf_op | source)
XLA Modules:
  0.0 44.0 jit_solution(9543761704368761528)
XLA Ops:
  0.0 43.2 %move_and_diffuse.1 = f32[4,16,16,128]{3,2,1,0:T(8,128)S(1)} custom-call(f32[1024,128]{1,0:T(8,128)} %bitcast.5, s32[64]{0:T(128)} %new_hbm.1, s32[64]{0:T(128)} %own_hbm.1), custom_call_target="tpu_custom_call" | custom-call | tf_op jit(solution)/shard_map/move_and_diffuse/pallas_call | solution.py:363
  43.2 0.8 %copy.6 = f32[4,16,16,128]{3,2,1,0:T(8,128)} copy(f32[4,16,16,128]{3,2,1,0:T(8,128)S(1)} %move_and_diffuse.1) | data formatting | bytes 1048576

commit v6 on v5

--- a/solution.py
+++ b/solution.py
@@ -274,7 +274,7 @@
             diff[part, :] = coefficient(grid[0, part, :])
             return c
 
-        lax.fori_loop(0, 18, diffusivity, 0, unroll=3)
+        lax.fori_loop(0, 18, diffusivity, 0, unroll=6)
         edges = [coefficient(edge) for edge in edges]
 
         def plane(x, c):
@@ -284,7 +284,7 @@
                 coef[s, n, pl.ds(pl.multiple_of(x * EDGE, EDGE), EDGE), :] = (0.5 * TIME_STEP) * (d + value)
             return c
 
-        lax.fori_loop(0, 16, plane, 0, unroll=UNROLL)
+        lax.fori_loop(0, 16, plane, 0, unroll=16)
 
     def section(s, k, copies, emit, start):
         grid = grids[s]

time: 44.1 us -> 44 us (level)
  no operation moved by 1% of the time
where the time goes in v6:
time: 44 us; the launch traced here: 43.9 us
  Pallas kernels  43.1 us (98%)
  local copies, waits for them, and re-layouts  0.8 us (2%)
    pallas_call x1, Pallas kernels, body(): pl.pallas_call(kernel, out_shape=jax.ShapeDtypeStruct((F, EDGE, EDGE, 128...  43.1 us

profile of v6, /device:TPU:1, one launch (start us, length us, event | category | flops | bytes accessed | tf_op | source)
XLA Modules:
  0.0 43.9 jit_solution(16784968228039442637)
XLA Ops:
  0.0 43.1 %move_and_diffuse.1 = f32[4,16,16,128]{3,2,1,0:T(8,128)S(1)} custom-call(f32[1024,128]{1,0:T(8,128)} %bitcast.5, s32[64]{0:T(128)} %new_hbm.1, s32[64]{0:T(128)} %own_hbm.1), custom_call_target="tpu_custom_call" | custom-call | tf_op jit(solution)/shard_map/move_and_diffuse/pallas_call | solution.py:363
  43.1 0.8 %copy.6 = f32[4,16,16,128]{3,2,1,0:T(8,128)} copy(f32[4,16,16,128]{3,2,1,0:T(8,128)S(1)} %move_and_diffuse.1) | data formatting | bytes 1048576
